TPU v7x, 256 devices: a whole 4x4x8 slice. The times are simulated.
256 devices in a mesh: aux: 32 (over y, x, core), vir: 8 (over z).
Axes of the slice: x: 4, y: 4, z: 8, core: 2. Of those that a mesh axis runs over, the one named last changes fastest.
Arguments:
- integrals: float32 [4096, 128, 1024], P('aux', None, 'vir'), may hold values from -0.024964112 to 0.024964112, as said below
- occupied_energy: float32 [128], P('aux'), may hold values from -3.5 to -2
- virtual_energy: float32 [1024], P('vir'), may hold values from 1.5 to 6
- right_side: float32 [1024, 128], P('vir', 'aux'), may hold values from -500 to 500
Outputs:
- solution: float32 [1024, 128], P('vir', 'aux')
- residual: float32 [1024, 128], P('vir', 'aux')
Inputs may be any that keep to these rules, and one draw needn't show every extreme that they name: Entries of the integrals are of order one over the fourth root of 536870912.
All inputs are finite; a program needn't handle non-finite values.
Results may differ from a plain program's by a relative error of at most 0.0003.
Values sent between devices are 32-bit elements; how exact they have to be, the bound alone decides.
A program may use at most 128 MiB of HBM per device.

v0:
```python
import jax
import jax.numpy as jnp
from jax import lax
from jax.sharding import PartitionSpec as P

ITERS = 3


HIGHEST = lax.Precision.HIGHEST


def squared_total(vector):
    return lax.psum(jnp.sum(vector * vector), ("aux", "vir"))


def on_device(integrals, occupied_energy, virtual_energy, right_side):
    energy_gap = virtual_energy[:, None] - occupied_energy[None, :]
    regrouped = lax.all_to_all(integrals, "vir", split_axis=0, concat_axis=2, tiled=True)
    aux_width = regrouped.shape[0]
    first_aux = lax.axis_index("vir") * aux_width
    solution = jnp.zeros_like(right_side)
    residual = right_side
    direction = right_side
    norm_now = squared_total(residual)
    for step in range(ITERS):
        trial_rows = lax.all_gather(direction, "aux", axis=1, tiled=True)
        trial_full = lax.all_gather(trial_rows, "vir", axis=0, tiled=True)
        coulomb_part = jnp.einsum("pia,ai->p", integrals, trial_rows, precision=HIGHEST)
        coulomb_all = lax.psum(coulomb_part, "vir")
        coulomb = lax.dynamic_slice_in_dim(coulomb_all, first_aux, aux_width)
        inter = jnp.einsum("pib,bj->pij", regrouped, trial_full, precision=HIGHEST)
        coulomb_term = jnp.einsum("pia,p->ai", regrouped, coulomb, precision=HIGHEST)
        exchange_term = jnp.einsum("pij,pja->ai", inter, regrouped, precision=HIGHEST)
        vir_rows = lax.psum_scatter(
            4.0 * coulomb_term - exchange_term, "vir", scatter_dimension=0, tiled=True
        )
        summed = lax.psum_scatter(vir_rows, "aux", scatter_dimension=1, tiled=True)
        image = energy_gap * direction + summed
        curvature = lax.psum(jnp.sum(direction * image), ("aux", "vir"))
        step_len = norm_now / curvature
        solution = solution + step_len * direction
        residual = residual - step_len * image
        if step + 1 < ITERS:
            norm_next = squared_total(residual)
            direction = residual + norm_next / norm_now * direction
            norm_now = norm_next
    return (solution, residual)


def solution(mesh):
    in_specs = (P("aux", None, "vir"), P("aux"), P("vir"), P("vir", "aux"))
    out_specs = (P("vir", "aux"), P("vir", "aux"))
    return jax.shard_map(
        on_device, mesh=mesh, in_specs=in_specs, out_specs=out_specs, check_vma=False
    )
```

profile of v0, /device:TPU:1, one launch (start us, length us, event | category | flops | bytes accessed | tf_op | source)
XLA Modules:
  0.0 1301.3 jit_solution(304148099080029103)
XLA Ops:
  7.2 0.0 copy-start.1
  7.2 9.0 all-to-all-start
  16.2 0.0 reduce-scatter.4.cloned.1.call-start
  16.2 25.3 %all-gather = f32[32,4,128]{2,1,0:T(4,128)S(1)} all-gather(f32[1,4,128]{2,1,0:T(4,128)S(1)} %bitcast.111), channel_id=1, replica_groups=mesh['aux'=32,'vir'=8] {'aux'}, dimensions={0}, use_global_device_ids=true | all-gather | bytes 67584 | tf_op jit(solution)/shard_map/all_gather | solution.py:26
  41.6 4.4 multiply_reduce_fusion.2
  46.0 161.1 %psum.64 = f32[128]{0:T(128)S(1)} all-reduce(f32[128]{0:T(128)S(1)} %multiply_reduce_fusion.2), channel_id=1, replica_groups=mesh['aux'=32,'vir'=8] {'vir'}, use_global_device_ids=true, to_apply=%region_2.0 | all-reduce | flops 128 | bytes 1024 | tf_op jit(solution)/shard_map/psum | solution.py:29
  207.1 19.8 %all_gather.19 = f32[1024,128]{0,1:T(8,128)S(1)} all-gather(f32[128,128]{0,1:T(8,128)S(1)} %bitcast.105), channel_id=1, replica_groups=mesh['aux'=32,'vir'=8] {'vir'}, dimensions={0}, use_global_device_ids=true | all-gather | bytes 589824 | tf_op jit(solution)/shard_map/all_gather | solution.py:27
  226.9 0.0 all-to-all-done
  226.9 13.1 %copy.40 = f32[8,16,128,128]{3,0,2,1:T(8,128)} copy(f32[8,16,128,128]{3,2,1,0:T(8,128)} %bitcast.8) | data formatting | bytes 16777216 | tf_op jit(solution)/shard_map/all_to_all | solution.py:18
  240.0 9.8 all_to_all.16
  249.8 9.2 fusion.14
  259.0 0.0 copy-start.4
  259.1 0.0 copy-start.2
  259.1 0.0 copy-start.3
  259.1 8.0 fusion.4
  267.1 5.5 fusion.7
  272.6 0.0 reduce-scatter.4.cloned.1.call-update
  272.6 0.0 all-reduce.8.cloned.1.call-start
  272.7 41.3 %reduce-scatter.4.cloned.1.call-done = f32[128,128]{0,1:T(8,128)} async-done(((f32[1024,128]{0,1:T(8,128)}), f32[128,128]{0,1:T(8,128)}) %reduce-scatter.4.cloned.1.call-update) | async-done | bytes 65552 | tf_op jit(solution)/shard_map/reduce_scatter | solution.py:34
  314.0 0.0 all-reduce.8.cloned.1.call-update
  314.0 0.0 reduce-scatter.6.cloned.1.call-start
  314.1 0.6 dynamic-slice
  315.3 112.8 %all-reduce.8.cloned.1.call-done = f32[128,128]{0,1:T(8,128)} async-done(((f32[128,128]{0,1:T(8,128)}), f32[128,128]{0,1:T(8,128)}) %all-reduce.8.cloned.1.call-update) | async-done | bytes 65552
  428.2 0.0 copy-done.2
  428.2 1.4 multiply_reduce_fusion.7
  429.5 74.9 %all-reduce.3 = (f32[]{:T(128)}, f32[]{:T(128)}) all-reduce(f32[]{:T(128)} %get-tuple-element.3, f32[]{:T(128)} %get-tuple-element.2), channel_id=1, replica_groups=mesh['aux'=32,'vir'=8] {'aux','vir'}, use_global_device_ids=true, to_apply=%region_1.0 | all-reduce | flops 2 | bytes 16 | tf_op jit(solution)/shard_map/psum | solution.py:13
  505.8 1.4 multiply_reduce_fusion.6
  507.1 73.5 %psum.66 = f32[]{:T(128)} all-reduce(f32[]{:T(128)} %get-tuple-element.8), channel_id=1, replica_groups=mesh['aux'=32,'vir'=8] {'aux','vir'}, use_global_device_ids=true, to_apply=%region_8.0 | all-reduce | flops 1 | bytes 8 | tf_op jit(solution)/shard_map/psum | solution.py:13
  582.0 24.2 %all-gather.1 = f32[32,4,128]{2,1,0:T(4,128)S(1)} all-gather(f32[1,4,128]{2,1,0:T(4,128)S(1)} %bitcast.110), channel_id=1, replica_groups=mesh['aux'=32,'vir'=8] {'aux'}, dimensions={0}, use_global_device_ids=true | all-gather | bytes 67584 | tf_op jit(solution)/shard_map/all_gather | solution.py:26
  606.2 4.4 multiply_reduce_fusion.1
  610.6 19.3 %all_gather.21 = f32[1024,128]{0,1:T(8,128)S(1)} all-gather(f32[128,128]{0,1:T(8,128)S(1)} %bitcast.109), channel_id=1, replica_groups=mesh['aux'=32,'vir'=8] {'vir'}, dimensions={0}, use_global_device_ids=true | all-gather | bytes 589824 | tf_op jit(solution)/shard_map/all_gather | solution.py:27
  629.9 12.3 psum.67
  642.2 12.2 fusion.2
  654.4 0.0 slice-start.1
  654.4 9.5 convolution_bitcast_fusion.1
  663.9 5.5 fusion.9
  669.5 0.0 reduce-scatter.6.cloned.1.call-update
  669.5 0.0 all-reduce.10.cloned.1.call-start
  669.5 38.1 %reduce-scatter.6.cloned.1.call-done = f32[128,128]{0,1:T(8,128)} async-done(((f32[1024,128]{0,1:T(8,128)}), f32[128,128]{0,1:T(8,128)}) %reduce-scatter.6.cloned.1.call-update) | async-done | bytes 65552 | tf_op jit(solution)/shard_map/reduce_scatter | solution.py:34
  707.7 0.0 all-reduce.10.cloned.1.call-update
  707.7 0.0 reduce-scatter.8.cloned.1.call-start
  707.7 114.1 %all-reduce.10.cloned.1.call-done = f32[128,128]{0,1:T(8,128)} async-done(((f32[128,128]{0,1:T(8,128)}), f32[128,128]{0,1:T(8,128)}) %all-reduce.10.cloned.1.call-update) | async-done | bytes 65552
  821.8 1.4 multiply_reduce_fusion.5
  823.2 74.9 %psum.68 = f32[]{:T(128)} all-reduce(f32[]{:T(128)} %multiply_reduce_fusion.5), channel_id=1, replica_groups=mesh['aux'=32,'vir'=8] {'aux','vir'}, use_global_device_ids=true, to_apply=%region_13.0 | all-reduce | flops 1 | bytes 8 | tf_op jit(solution)/shard_map/psum | solution.py:39
  899.4 1.4 multiply_reduce_fusion.4
  900.7 73.5 %psum.69 = f32[]{:T(128)} all-reduce(f32[]{:T(128)} %get-tuple-element.6), channel_id=1, replica_groups=mesh['aux'=32,'vir'=8] {'aux','vir'}, use_global_device_ids=true, to_apply=%region_15.0 | all-reduce | flops 1 | bytes 8 | tf_op jit(solution)/shard_map/psum | solution.py:13
  975.6 24.1 %all-gather.2 = f32[32,4,128]{2,1,0:T(4,128)S(1)} all-gather(f32[1,4,128]{2,1,0:T(4,128)S(1)} %fusion.25), channel_id=1, replica_groups=mesh['aux'=32,'vir'=8] {'aux'}, dimensions={0}, use_global_device_ids=true | all-gather | bytes 67584 | tf_op jit(solution)/shard_map/all_gather | solution.py:26
  999.7 4.4 multiply_reduce_fusion
  1004.2 19.3 %all_gather.23 = f32[1024,128]{0,1:T(8,128)S(1)} all-gather(f32[128,128]{0,1:T(8,128)S(1)} %bitcast.107), channel_id=1, replica_groups=mesh['aux'=32,'vir'=8] {'vir'}, dimensions={0}, use_global_device_ids=true | all-gather | bytes 589824 | tf_op jit(solution)/shard_map/all_gather | solution.py:27
  1023.4 12.5 psum.70
  1036.0 12.2 fusion
  1048.2 0.0 slice-start.3
  1048.2 9.4 convolution_bitcast_fusion
  1057.6 0.0 slice-done.2
  1057.6 0.0 slice-done.3
  1057.6 5.5 fusion.11
  1063.1 0.0 reduce-scatter.8.cloned.1.call-update
  1063.1 0.0 all-reduce.12.cloned.1.call-start
  1063.2 38.2 %reduce-scatter.8.cloned.1.call-done = f32[128,128]{0,1:T(8,128)} async-done(((f32[1024,128]{0,1:T(8,128)}), f32[128,128]{0,1:T(8,128)}) %reduce-scatter.8.cloned.1.call-update) | async-done | bytes 65552 | tf_op jit(solution)/shard_map/reduce_scatter | solution.py:34
  1101.3 0.0 all-reduce.12.cloned.1.call-update
  1101.3 114.0 %all-reduce.12.cloned.1.call-done = f32[128,128]{0,1:T(8,128)} async-done(((f32[128,128]{0,1:T(8,128)}), f32[128,128]{0,1:T(8,128)}) %all-reduce.12.cloned.1.call-update) | async-done | bytes 65552
  1215.4 1.4 multiply_reduce_fusion.3
  1216.7 74.9 %psum.71 = f32[]{:T(128)} all-reduce(f32[]{:T(128)} %multiply_reduce_fusion.3), channel_id=1, replica_groups=mesh['aux'=32,'vir'=8] {'aux','vir'}, use_global_device_ids=true, to_apply=%region_20.0 | all-reduce | flops 1 | bytes 8 | tf_op jit(solution)/shard_map/psum | solution.py:39
  1292.9 1.3 multiply_subtract_fusion
  (13 shorter events, 0.0 us)
Async XLA Ops:
  7.2 9.1 copy-start.1
  7.2 219.7 %all-to-all-start = ((f32[128,128,128]{2,1,0:T(8,128)}), f32[128,128,128]{2,1,0:T(8,128)}, u32[]{:S(2)}, u32[]{:S(2)}) async-start(f32[128,128,128]{2,1,0:T(8,128)} %param.4), calls=%async_computation | async-start | bytes 16777216 | tf_op jit(solution)/shard_map/all_to_all | solution.py:18
  16.2 297.8 %reduce-scatter.4.cloned.1.call-start = ((), (), s32[]{:S(2)}) async-start(), calls=%async_computation.4 | async-start | bytes 589824 | tf_op jit(solution)/shard_map/reduce_scatter | solution.py:34
  249.8 9.2 copy-start
  259.0 55.0 %copy-start.4 = (u32[256]{0:T(256)S(1)}, u32[256]{0:T(256)}, u32[]{:S(2)}) copy-start(u32[256]{0:T(256)} %constant.21) | copy-start | bytes 3076
  259.1 169.1 %copy-start.2 = (f32[4]{0:T(128)S(1)}, f32[4]{0:T(128)}, u32[]{:S(2)}) copy-start(f32[4]{0:T(128)} %param.5) | copy-start | bytes 52
  259.1 169.1 %copy-start.3 = (f32[128]{0:T(128)S(1)}, f32[128]{0:T(128)}, u32[]{:S(2)}) copy-start(f32[128]{0:T(128)} %param.6) | copy-start | bytes 1540
  272.6 155.5 %all-reduce.8.cloned.1.call-start = ((), (), s32[]{:S(2)}) async-start(), calls=%async_computation.7 | async-start | bytes 131072
  314.0 393.7 %reduce-scatter.6.cloned.1.call-start = ((), (), s32[]{:S(2)}) async-start(), calls=%async_computation.5 | async-start | bytes 589824 | tf_op jit(solution)/shard_map/reduce_scatter | solution.py:34
  642.2 21.7 %slice-start = ((s8[8388608]{0:T(1024)(128)(4,1)}), s8[4194304]{0:T(1024)(128)(4,1)S(1)}, s32[]{:S(2)}) async-start(s8[8388608]{0:T(1024)(128)(4,1)} %bitcast.99), calls=%async_computation.10 | async-start | bytes 8388608
  654.4 9.5 slice-start.1
  669.5 152.3 %all-reduce.10.cloned.1.call-start = ((), (), s32[]{:S(2)}) async-start(), calls=%async_computation.8 | async-start | bytes 131072
  707.7 393.6 %reduce-scatter.8.cloned.1.call-start = ((), (), s32[]{:S(2)}) async-start(), calls=%async_computation.6 | async-start | bytes 589824 | tf_op jit(solution)/shard_map/reduce_scatter | solution.py:34
  1036.0 21.6 %slice-start.2 = ((s8[8388608]{0:T(1024)(128)(4,1)}), s8[4194304]{0:T(1024)(128)(4,1)S(1)}, s32[]{:S(2)}) async-start(s8[8388608]{0:T(1024)(128)(4,1)} %bitcast.101), calls=%async_computation.12 | async-start | bytes 8388608
  1048.2 9.4 slice-start.3
  1063.1 152.3 %all-reduce.12.cloned.1.call-start = ((), (), s32[]{:S(2)}) async-start(), calls=%async_computation.9 | async-start | bytes 131072
Sparse Core Ops, SparseCore 0:
  272.8 41.1 reduce-scatter.3
  317.2 110.8 all-reduce.7
  669.6 38.0 reduce-scatter.5
  710.8 110.9 all-reduce.9
  1063.2 38.0 reduce-scatter.7
  1104.4 110.9 all-reduce.11
where the time goes:
time: 1310 us; the launch traced here: 1300 us
  blocking collectives  690 us (53%)
  waiting for transfers between devices  459 us (35%)
  matrix products  77 us (6%)
  local copies, waits for them, and re-layouts  23.5 us (2%)
  between operations  21.8 us (2%)
  other arithmetic  21.4 us (2%)
    unnamed x9, waiting for transfers between devices  341 us
    psum x3, blocking collectives, squared_total(): return lax.psum(jnp.sum(vector * vector), ('aux', 'vir'))  222 us
    psum x3, blocking collectives, on_device(): coulomb_all = lax.psum(coulomb_part, 'vir')  186 us
    psum x2, blocking collectives, on_device(): curvature = lax.psum(jnp.sum(direction * image), ('aux', 'vir'))  150 us
    reduce_scatter x3, waiting for transfers between devices, on_device(): lax.psum_scatter(4.0 * coulomb_term - exchange_term, 'vir', scatter_dimen...  118 us
    all_gather x3, blocking collectives, on_device(): trial_rows = lax.all_gather(direction, 'aux', axis=1, tiled=True)  73.6 us
    all_gather x3, blocking collectives, on_device(): trial_full = lax.all_gather(trial_rows, 'vir', axis=0, tiled=True)  58.3 us
    dot_general x3, matrix products, on_device(): jnp.einsum('pia,p->ai', regrouped, coulomb, precision=HIGHEST)  32.4 us
  transfers between devices with their start and end apart: 7, of which 6 were waited for; matrix products, arithmetic and copies ran while one was open for 0% of the time, Pallas kernels for 0%

commit v1 on v0

v1 whole, which is shorter than its diff:
```python
import functools

import jax
import jax.numpy as jnp
from jax import lax
from jax.experimental import pallas as pl
from jax.experimental.pallas import tpu as pltpu
from jax.sharding import PartitionSpec as P

ITERS = 3
NZ = 8
NM = 16
NP = 16
O = 128
V = 1024
W = V + 128
MESH = pl.DeviceIdType.MESH
F32 = jnp.float32
BF16 = jnp.bfloat16
ARRIVAL = (4, 3, 5, 2, 6, 1, 7)


def total(x):
    return jnp.sum(jnp.sum(x, axis=0, keepdims=True), axis=1, keepdims=True)


def split(x):
    high = x.astype(BF16)
    return high, (x - high.astype(F32)).astype(BF16)


def kernel(
    ints, occ, vir, rhs, sol, res,
    recv, bhi, blo, d, r, img, part, cbuf, xbuf, zsend, zbuf, g, g2, gap, x, d2, zs, rr, fin,
    a2a_s, a2a_r, loc, iz_s, iz_r, ic, agz_s, agz_r, agx_s, agx_r, agc_s, agc_r,
    rsc, rsx_s, rsx_r, rsz_s, rsz_r, fs,
):
    a = lax.axis_index("aux")
    z = lax.axis_index("vir")
    c = lax.rem(a, 2)
    m = lax.div(a, 2)
    owner = lax.div(m, 8) == c
    partner = (2 * m + 1 - c, z)

    def at_z(k):
        return (a, lax.rem(z + k + NZ, NZ))

    def at_m(chip):
        return (2 * chip + c, z)

    def remote(src, dst, send, recv_sem, dev):
        return pltpu.make_async_remote_copy(
            src_ref=src, dst_ref=dst, send_sem=send, recv_sem=recv_sem, device_id=dev, device_id_type=MESH
        )

    def rows(ref, chip, count=8):
        return ref.at[pl.ds(pl.multiple_of(8 * chip, 8), count)]

    barrier = pltpu.get_barrier_semaphore()
    pl.semaphore_signal(barrier, inc=1, device_id=partner, device_id_type=MESH)
    for k in range(1, NZ):
        pl.semaphore_signal(barrier, inc=1, device_id=at_z(k), device_id_type=MESH)
    for j in range(1, NM):
        pl.semaphore_signal(barrier, inc=1, device_id=at_m(lax.rem(m + j, NM)), device_id_type=MESH)

    row = lax.broadcasted_iota(jnp.int32, (8, 128), 0)
    mine = lax.div(row, 4) == c
    occ_rows = jnp.zeros((8, 128), F32)
    for i in range(4):
        occ_rows = jnp.where(lax.rem(row, 4) == i, occ[i], occ_rows)
    own = rhs[...]
    g[:, 0:128] = jnp.where(mine, jnp.concatenate([own, own], axis=0), 0.0)
    g[:, V:W] = jnp.where(mine, jnp.broadcast_to(vir[...], (8, 128)) - occ_rows, 0.0)

    pl.semaphore_wait(barrier, 1 + NZ - 1 + NM - 1)

    def init_z(k):
        return remote(g.at[:, 0:128], g.at[:, k * 128:(k + 1) * 128], iz_s.at[k], iz_r.at[k], at_z(k))

    def exchange(k):
        to = lax.rem(z + k, NZ)
        return remote(ints.at[pl.ds(to * NP, NP)], recv.at[k], a2a_s.at[k], a2a_r.at[k], (a, to))

    for k in range(1, NZ):
        init_z(k).start()
    for k in ARRIVAL:
        exchange(k).start()
    local = pltpu.make_async_copy(ints.at[pl.ds(z * NP, NP)], recv.at[0], loc)
    local.start()

    def spread():
        def to_chip(j):
            return remote(
                rows(img, m), rows(img, m), agx_s.at[j], agx_r.at[lax.rem(m, 8)], at_m(lax.rem(m + j, NM))
            )

        def to_partner(t):
            block = rows(img, 8 * c + t)
            return remote(block, block, agc_s.at[t], agc_r.at[t], partner)

        def from_partner(t):
            block = rows(img, 8 * (1 - c) + t)
            return remote(block, block, agc_s.at[t], agc_r.at[t], partner)

        @pl.when(owner)
        def _():
            for j in range(1, NM):
                to_chip(j).start()
            to_partner(lax.rem(m, 8)).start()

        for t in range(8):
            @pl.when(8 * c + t != m)
            def _():
                block = rows(img, 8 * c + t)
                remote(block, block, agx_s.at[0], agx_r.at[t], partner).wait_recv()
                to_partner(t).start()

        for t in range(8):
            from_partner(t).wait_recv()
        for t in range(8):
            to_partner(t).wait_send()

        @pl.when(owner)
        def _():
            for j in range(1, NM):
                to_chip(j).wait_send()

    for k in range(1, NZ):
        init_z(k).wait_recv()
    swap = remote(g, g2, ic.at[0], ic.at[1], partner)
    swap.start()
    swap.wait_recv()
    gap[...] = g[:, V:W] + g2[:, V:W]

    @pl.when(owner)
    def _():
        rows(img, m)[...] = g[:, 0:V] + g2[:, 0:V]

    spread()
    swap.wait_send()
    for k in range(1, NZ):
        init_z(k).wait_send()

    first = img[...]
    d[...] = first
    r[...] = first
    rr[...] = jnp.broadcast_to(total(first * first), (8, 128))
    x[...] = jnp.zeros((8, 128), F32)

    def convert(k):
        def body(p, carry):
            high, low = split(recv[k, p])
            at = pl.ds(pl.multiple_of(p * 128, 128), 128)
            bhi[at, k * 128:(k + 1) * 128] = high
            blo[at, k * 128:(k + 1) * 128] = low
            return carry

        lax.fori_loop(0, NP, body, 0)

    local.wait()
    convert(0)
    for k in ARRIVAL:
        exchange(k).wait_recv()
        convert(k)

    def apply_local():
        high, low = split(d[...])
        d2[0:128, :] = high
        d2[128:256, :] = low
        eye = lax.broadcasted_iota(jnp.int32, (128, 128), 0) == lax.broadcasted_iota(jnp.int32, (128, 128), 1)
        contract = (((1,), (1,)), ((), ()))

        def inter(n, carry):
            at = pl.ds(pl.multiple_of(n * 512, 512), 512)
            both = lax.dot_general(bhi[at, :], d2[...], contract, preferred_element_type=F32)
            rest = lax.dot_general(blo[at, :], d2[0:128, :], contract, preferred_element_type=F32)
            y = both[:, 0:128] + both[:, 128:256] + rest
            for q in range(4):
                block = y[q * 128:(q + 1) * 128, :]
                coulomb = total(jnp.where(eye, block, 0.0))
                zh, zl = split(jnp.where(eye, 4.0 * coulomb, 0.0) - block)
                cols = pl.ds(pl.multiple_of(n * 512 + q * 128, 128), 128)
                zs[0:128, cols] = zh
                zs[128:256, cols] = zl
            return carry

        lax.fori_loop(0, NP // 4, inter, 0)

        def outer(n, carry):
            cols = pl.ds(pl.multiple_of(n * 256, 256), 256)
            both = jnp.dot(zs[...], bhi[:, cols], preferred_element_type=F32)
            rest = jnp.dot(zs[0:128, :], blo[:, cols], preferred_element_type=F32)
            part[:, cols] = both[0:128] + both[128:256] + rest
            return carry

        lax.fori_loop(0, V // 256, outer, 0)

    def reduce(width, tail):
        theirs = rows(part, 8 * (1 - c), 64).at[:, 0:width]
        pair = remote(theirs, cbuf.at[:, 0:width], rsc.at[0], rsc.at[1], partner)
        pair.start()
        pair.wait_recv()
        half = rows(part, 8 * c, 64)
        half[:, 0:width] = half[:, 0:width] + cbuf[:, 0:width]

        def to_chip(t):
            chip = 8 * c + t
            j = lax.rem(chip - m + NM, NM)
            return remote(
                rows(part, chip).at[:, 0:width], xbuf.at[j, :, 0:width], rsx_s.at[t], rsx_r.at[j], at_m(chip)
            )

        for t in range(8):
            @pl.when(8 * c + t != m)
            def _():
                to_chip(t).start()

        @pl.when(owner)
        def _():
            acc = rows(part, m)[:, 0:width]
            for j in range(1, NM):
                slot = xbuf.at[j, :, 0:width]
                remote(slot, slot, rsx_s.at[0], rsx_r.at[j], partner).wait_recv()
                acc = acc + xbuf[j, :, 0:width]
            wide = 128 + width - V

            def to_z(k):
                return remote(
                    zsend.at[k, :, 0:wide], zbuf.at[k, :, 0:wide], rsz_s.at[k], rsz_r.at[k], at_z(-k)
                )

            for k in range(1, NZ):
                zsend[k, :, 0:128] = acc[:, k * 128:(k + 1) * 128]
                if wide > 128:
                    zsend[k, :, 128:256] = acc[:, V:W]
                to_z(k).start()
            tile = acc[:, 0:128]
            scalar = acc[:, V:W] if wide > 128 else None
            for k in range(1, NZ):
                to_z(k).wait_recv()
                tile = tile + zbuf[k, :, 0:128]
                if wide > 128:
                    scalar = scalar + zbuf[k, :, 128:256]
            tail(gap[...] * rows(d, m)[:, 0:128] + tile, scalar)
            for k in range(1, NZ):
                to_z(k).wait_send()

        for t in range(8):
            @pl.when(8 * c + t != m)
            def _():
                to_chip(t).wait_send()
        pair.wait_send()

    def iterate(step, carry):
        apply_local()

        def tail(tile, scalar):
            def to_z(k):
                return remote(
                    rows(img, m).at[:, 0:128], rows(img, m).at[:, k * 128:(k + 1) * 128],
                    agz_s.at[k], agz_r.at[k], at_z(k),
                )

            rows(img, m)[:, 0:128] = tile
            for k in range(1, NZ):
                to_z(k).start()
            for k in range(1, NZ):
                to_z(k).wait_recv()
            for k in range(1, NZ):
                to_z(k).wait_send()

        reduce(V, tail)
        spread()
        image, trial = img[...], d[...]
        old = rr[0:1, 0:1]
        alpha = old / total(trial * image)
        x[...] = x[...] + alpha * rows(d, m)[:, 0:128]
        left = r[...] - alpha * image
        new = total(left * left)
        r[...] = left
        d[...] = left + (new / old) * trial
        rr[...] = jnp.broadcast_to(new, (8, 128))
        return carry

    lax.fori_loop(0, ITERS - 1, iterate, 0)

    apply_local()
    own_d = rows(d, m)[:, 0:128]
    own_gap = total(gap[...] * own_d * own_d)
    curve = total(d[...] * part[:, 0:V]) + jnp.where(owner, own_gap, jnp.zeros_like(own_gap))
    part[:, V:W] = jnp.broadcast_to(curve, (128, 128))

    def hand(ref):
        return remote(ref, ref, fs.at[0], fs.at[1], partner)

    def last(tile, scalar):
        fin[:, 0:128] = tile
        fin[:, 128:256] = scalar
        hand(fin).start()
        hand(fin).wait_send()

    reduce(W, last)

    @pl.when(jnp.logical_not(owner))
    def _():
        hand(fin).wait_recv()

    alpha = rr[...] / fin[:, 128:256]
    answer = x[...] + alpha * rows(d, m)[:, 0:128]
    left = rows(r, m)[:, 0:128] - alpha * fin[:, 0:128]
    lower = c == 0
    sol[...] = jnp.where(lower, answer[0:4], answer[4:8])
    res[...] = jnp.where(lower, left[0:4], left[4:8])

    for k in ARRIVAL:
        exchange(k).wait_send()


def on_device(integrals, occupied_energy, virtual_energy, right_side):
    dma = pltpu.SemaphoreType.DMA
    vmem = pl.BlockSpec(memory_space=pltpu.VMEM)
    out = jax.ShapeDtypeStruct((4, 128), F32)
    answer, left = pl.pallas_call(
        kernel,
        out_shape=(out, out),
        in_specs=[pl.BlockSpec(memory_space=pl.ANY), pl.BlockSpec(memory_space=pltpu.SMEM), vmem, vmem],
        out_specs=(vmem, vmem),
        scratch_shapes=[
            pltpu.VMEM((NZ, NP, 128, 128), F32),
            pltpu.VMEM((NP * O, V), BF16),
            pltpu.VMEM((NP * O, V), BF16),
            pltpu.VMEM((O, V), F32),
            pltpu.VMEM((O, V), F32),
            pltpu.VMEM((O, V), F32),
            pltpu.VMEM((O, W), F32),
            pltpu.VMEM((64, W), F32),
            pltpu.VMEM((NM, 8, W), F32),
            pltpu.VMEM((NZ, 8, 256), F32),
            pltpu.VMEM((NZ, 8, 256), F32),
            pltpu.VMEM((8, W), F32),
            pltpu.VMEM((8, W), F32),
            pltpu.VMEM((8, 128), F32),
            pltpu.VMEM((8, 128), F32),
            pltpu.VMEM((256, V), BF16),
            pltpu.VMEM((256, NP * O), BF16),
            pltpu.VMEM((8, 128), F32),
            pltpu.VMEM((8, 256), F32),
            dma((NZ,)), dma((NZ,)), dma(()),
            dma((NZ,)), dma((NZ,)), dma((2,)),
            dma((NZ,)), dma((NZ,)), dma((NM,)), dma((8,)), dma((8,)), dma((8,)),
            dma((2,)), dma((8,)), dma((NM,)), dma((NZ,)), dma((NZ,)), dma((2,)),
        ],
        compiler_params=pltpu.CompilerParams(
            collective_id=0, has_side_effects=True, vmem_limit_bytes=60 << 20
        ),
        name="solve",
    )(integrals, occupied_energy, virtual_energy.reshape(1, 128), right_side.T)
    return answer.T, left.T


def solution(mesh):
    in_specs = (P("aux", None, "vir"), P("aux"), P("vir"), P("vir", "aux"))
    out_specs = (P("vir", "aux"), P("vir", "aux"))
    return jax.shard_map(
        on_device, mesh=mesh, in_specs=in_specs, out_specs=out_specs, check_vma=False
    )
```

time: 1310 us -> 282 us (0.22)
  blocking collectives: 690 us -> 0 us
  waiting for transfers between devices: 459 us -> 0 us
  Pallas kernels: 0 us -> 278 us
  matrix products: 77 us -> 0 us
  other arithmetic: 21.4 us -> 0 us
  between operations: 21.8 us -> 0.64 us
  local copies, waits for them, and re-layouts: 23.5 us -> 2.48 us
    psum x8 -> x0, blocking collectives: 558 us -> none  [the longest x3 222 us: squared_total(): return lax.psum(jnp.sum(vector * vector), ('aux', 'vir'))]
    unnamed x9 -> x0, waiting for transfers between devices: 341 us -> none
    pallas_call x0 -> x1, Pallas kernels: none -> 278 us  [on_device(): pl.pallas_call(kernel, out_shape=(out, out), in_specs=[pl.BlockSpec(memor...]
    all_gather x6 -> x0, blocking collectives: 132 us -> none  [the longest x3 73.6 us: on_device(): trial_rows = lax.all_gather(direction, 'aux', axis=1, tiled=True)]
    reduce_scatter x3 -> x0, waiting for transfers between devices: 118 us -> none  [on_device(): lax.psum_scatter(4.0 * coulomb_term - exchange_term, 'vir', scatter_dimen...]
    dot_general x9 -> x0, matrix products: 77 us -> none  [the longest x3 32.4 us: on_device(): jnp.einsum('pia,p->ai', regrouped, coulomb, precision=HIGHEST)]
    all_to_all x2 -> x0, local copies, waits for them, and re-layouts: 22.9 us -> none  [on_device(): lax.all_to_all(integrals, 'vir', split_axis=0, concat_axis=2, tiled=True)]
    dot_general x3 -> x0, other arithmetic: 13.3 us -> none  [on_device(): jnp.einsum('pia,ai->p', integrals, trial_rows, precision=HIGHEST)]
  transfers between devices with their start and end apart: 7 -> 0, of which waited for: 6 -> 0; matrix products, arithmetic and copies ran while one was open for 0% -> 0% of each run, Pallas kernels for 0% -> 0%
where the time goes in v1:
time: 282 us; the launch traced here: 281 us
  Pallas kernels  278 us (99%)
    pallas_call x1, Pallas kernels, on_device(): pl.pallas_call(kernel, out_shape=(out, out), in_specs=[pl.BlockSpec(memor...  278 us

profile of v1, /device:TPU:1, one launch (start us, length us, event | category | flops | bytes accessed | tf_op | source)
XLA Modules:
  0.0 281.4 jit_solution(12550553404189078013)
XLA Ops:
  0.6 278.3 %solve.1 = (f32[4,128]{1,0:T(4,128)}, f32[4,128]{1,0:T(4,128)}) custom-call(f32[128,128,128]{2,1,0:T(8,128)} %ints.1, f32[4]{0:T(128)} %occ.1, f32[1,128]{1,0:T(1,128)} %bitcast.7, f32[4,128]{1,0:T(4,128)} %bitcast.4), custom_call_target="tpu_custom_call" | custom-call | tf_op jit(solution)/shard_map/solve/pallas_call | solution.py:323
  279.0 1.2 copy.8
  280.2 1.2 copy.9

commit v2 on v1

v2 whole, which is shorter than its diff:
```python
import functools

import jax
import jax.numpy as jnp
from jax import lax
from jax.experimental import pallas as pl
from jax.experimental.pallas import tpu as pltpu
from jax.sharding import PartitionSpec as P

ITERS = 3
NZ = 8
NM = 16
NP = 16
O = 128
V = 1024
W = V + 128
MESH = pl.DeviceIdType.MESH
F32 = jnp.float32
BF16 = jnp.bfloat16
SHIFT = (0, 1, -1, 2, -2, 3, -3, 4)
ISSUE = (7, 5, 6, 3, 4, 1, 2)
HALF = 512
CHUNKS = 4
NC = NP // CHUNKS
NEAR, FAR = 0, 1


def total(x):
    return jnp.sum(jnp.sum(x, axis=0, keepdims=True), axis=1, keepdims=True)


def split(x):
    high = x.astype(BF16)
    return high, (x - high.astype(F32)).astype(BF16)


def kernel(
    ints, occ, vir, rhs, out,
    recv, bhi, blo, d, r, img, part, cbuf, xbuf, zsend, zbuf, sbuf, g, g2, gap, x, d2, zs, rr, fin,
    a2a_s, a2a_r, loc, iz_s, iz_r, ic, agz_s, agz_r, agx_s, agx_r, agc_s, agc_r,
    rsc_s, rsc_r, rsx_s, rsx_r, rsz_s, rsz_r, sc_s, sc_r, fs,
):
    a = lax.axis_index("aux")
    z = lax.axis_index("vir")
    c = lax.rem(a, 2)
    m = lax.div(a, 2)
    owner = lax.div(m, 8) == c
    partner = (2 * m + 1 - c, z)

    def at_z(k):
        return (a, lax.rem(z + k + NZ, NZ))

    def at_m(chip):
        return (2 * chip + c, z)

    def remote(src, dst, send, recv_sem, dev):
        return pltpu.make_async_remote_copy(
            src_ref=src, dst_ref=dst, send_sem=send, recv_sem=recv_sem, device_id=dev, device_id_type=MESH
        )

    def rows(ref, chip, count=8):
        return ref.at[pl.ds(pl.multiple_of(8 * chip, 8), count)]

    barrier = pltpu.get_barrier_semaphore()
    pl.semaphore_signal(barrier, inc=1, device_id=partner, device_id_type=MESH)
    for k in range(1, NZ):
        pl.semaphore_signal(barrier, inc=1, device_id=at_z(k), device_id_type=MESH)
    for j in range(1, NM):
        pl.semaphore_signal(barrier, inc=1, device_id=at_m(lax.rem(m + j, NM)), device_id_type=MESH)

    row = lax.broadcasted_iota(jnp.int32, (8, 128), 0)
    mine = lax.div(row, 4) == c
    occ_rows = jnp.zeros((8, 128), F32)
    for i in range(4):
        occ_rows = jnp.where(lax.rem(row, 4) == i, occ[i], occ_rows)
    own = rhs[...]
    g[:, 0:128] = jnp.where(mine, jnp.concatenate([own, own], axis=0), 0.0)
    g[:, V:W] = jnp.where(mine, jnp.broadcast_to(vir[...], (8, 128)) - occ_rows, 0.0)

    pl.semaphore_wait(barrier, 1 + NZ - 1 + NM - 1)

    def init_z(q):
        return remote(g.at[:, 0:128], g.at[:, q * 128:(q + 1) * 128], iz_s.at[q], iz_r.at[q], at_z(SHIFT[q]))

    def exchange(q, n):
        to = lax.rem(z + SHIFT[q] + NZ, NZ)
        return remote(
            ints.at[pl.ds(to * NP + n * NC, NC)], recv.at[q, pl.ds(n * NC, NC)], a2a_s.at[q, n], a2a_r.at[q, n], (a, to)
        )

    for q in range(1, NZ):
        init_z(q).start()
    for n in range(CHUNKS):
        for q in ISSUE:
            exchange(q, n).start()
    local = pltpu.make_async_copy(ints.at[pl.ds(z * NP, NP)], recv.at[0], loc)
    local.start()

    def spread(ready):
        def piece(chip, h):
            return rows(img, chip).at[:, h * HALF:(h + 1) * HALF]

        def to_chip(j, h):
            return remote(
                piece(m, h), piece(m, h), agx_s.at[h, j], agx_r.at[h, lax.rem(m, 8)], at_m(lax.rem(m + j, NM))
            )

        def to_partner(t, h):
            block = piece(8 * c + t, h)
            return remote(block, block, agc_s.at[h, t], agc_r.at[h, t], partner)

        def from_partner(t, h):
            block = piece(8 * (1 - c) + t, h)
            return remote(block, block, agc_s.at[h, t], agc_r.at[h, t], partner)

        @pl.when(owner)
        def _():
            for h in (NEAR, FAR):
                ready(h)
                for j in range(1, NM):
                    to_chip(j, h).start()
                to_partner(lax.rem(m, 8), h).start()

        for h in (NEAR, FAR):
            for t in range(8):
                @pl.when(8 * c + t != m)
                def _():
                    block = piece(8 * c + t, h)
                    remote(block, block, agx_s.at[0, 0], agx_r.at[h, t], partner).wait_recv()
                    to_partner(t, h).start()

        for h in (NEAR, FAR):
            for t in range(8):
                from_partner(t, h).wait_recv()
        for h in (NEAR, FAR):
            for t in range(8):
                to_partner(t, h).wait_send()

        @pl.when(owner)
        def _():
            for h in (NEAR, FAR):
                for j in range(1, NM):
                    to_chip(j, h).wait_send()

    for q in range(1, NZ):
        init_z(q).wait_recv()
    swap = remote(g, g2, ic.at[0], ic.at[1], partner)
    swap.start()
    swap.wait_recv()
    gap[...] = g[:, V:W] + g2[:, V:W]

    @pl.when(owner)
    def _():
        rows(img, m)[...] = g[:, 0:V] + g2[:, 0:V]

    spread(lambda h: None)
    swap.wait_send()
    for q in range(1, NZ):
        init_z(q).wait_send()

    first = img[...]
    d[...] = first
    r[...] = first
    rr[...] = jnp.broadcast_to(total(first * first), (8, 128))
    x[...] = jnp.zeros((8, 128), F32)

    def set_trial():
        high, low = split(d[...])
        d2[0:128, :] = high
        d2[128:256, :] = low

    def inter(n, carry):
        eye = lax.broadcasted_iota(jnp.int32, (128, 128), 0) == lax.broadcasted_iota(jnp.int32, (128, 128), 1)
        contract = (((1,), (1,)), ((), ()))
        size = NC * O
        at = pl.ds(pl.multiple_of(n * size, size), size)
        both = lax.dot_general(bhi[at, :], d2[...], contract, preferred_element_type=F32)
        rest = lax.dot_general(blo[at, :], d2[0:128, :], contract, preferred_element_type=F32)
        y = both[:, 0:128] + both[:, 128:256] + rest
        for i in range(NC):
            block = y[i * 128:(i + 1) * 128, :]
            coulomb = total(jnp.where(eye, block, 0.0))
            zh, zl = split(jnp.where(eye, 4.0 * coulomb, 0.0) - block)
            cols = pl.ds(pl.multiple_of(n * size + i * 128, 128), 128)
            zs[0:128, cols] = zh
            zs[128:256, cols] = zl
        return carry

    def outer(h):
        def body(n, carry):
            cols = pl.ds(pl.multiple_of(h * HALF + n * 256, 256), 256)
            to = pl.ds(pl.multiple_of(h * (HALF + 128) + n * 256, 128), 256)
            both = jnp.dot(zs[...], bhi[:, cols], preferred_element_type=F32)
            rest = jnp.dot(zs[0:128, :], blo[:, cols], preferred_element_type=F32)
            part[:, to] = both[0:128] + both[128:256] + rest
            return carry

        lax.fori_loop(0, HALF // 256, body, 0)

    set_trial()
    local.wait()

    def arrive(n, carry):
        for q in ISSUE:
            exchange(q, n).wait_recv()

        def body(i, carry):
            p = n * NC + i
            at = pl.ds(pl.multiple_of(p * 128, 128), 128)
            for q in range(NZ):
                high, low = split(recv[q, p])
                bhi[at, q * 128:(q + 1) * 128] = high
                blo[at, q * 128:(q + 1) * 128] = low
            return carry

        lax.fori_loop(0, NC, body, 0)
        return inter(n, carry)

    lax.fori_loop(0, CHUNKS, arrive, 0)

    def span(h, scalar):
        if h == FAR:
            return slice(HALF + 128, W)
        return slice(0, HALF + 128 if scalar else HALF)

    def reduce(before, tail, scalar):
        def pair(h):
            cols = span(h, scalar)
            theirs = rows(part, 8 * (1 - c), 64).at[:, cols]
            return remote(theirs, cbuf.at[:, cols], rsc_s.at[h], rsc_r.at[h], partner)

        def to_chip(t, h):
            chip = 8 * c + t
            j = lax.rem(chip - m + NM, NM)
            cols = span(h, scalar)
            return remote(
                rows(part, chip).at[:, cols], xbuf.at[j, :, cols], rsx_s.at[h, t], rsx_r.at[h, j], at_m(chip)
            )

        def to_z(q):
            return remote(zsend.at[q], zbuf.at[q], rsz_s.at[q], rsz_r.at[q], at_z(-SHIFT[q]))

        def scalar_z(q):
            return remote(zsend.at[0], sbuf.at[q], sc_s.at[q], sc_r.at[q], at_z(-SHIFT[q]))

        for h in (FAR, NEAR):
            outer(h)
            if h == NEAR:
                before()
            pair(h).start()
        for h in (FAR, NEAR):
            pair(h).wait_recv()
            cols = span(h, scalar)
            half = rows(part, 8 * c, 64)
            half[:, cols] = half[:, cols] + cbuf[:, cols]
            for t in range(8):
                @pl.when(8 * c + t != m)
                def _():
                    to_chip(t, h).start()

        @pl.when(owner)
        def _():
            for h in (FAR, NEAR):
                cols = span(h, scalar)
                acc = rows(part, m)[:, cols]
                for j in range(1, NM):
                    slot = xbuf.at[j, :, cols]
                    remote(slot, slot, rsx_s.at[0, 0], rsx_r.at[h, j], partner).wait_recv()
                    acc = acc + xbuf[j, :, cols]
                if scalar and h == NEAR:
                    zsend[0] = acc[:, HALF:HALF + 128]
                    for q in range(NZ - 1, 0, -1):
                        scalar_z(q).start()
                for q in range(4 * h + 3, 4 * h - 1, -1):
                    if q > 0:
                        zsend[q] = acc[:, (q - 4 * h) * 128:(q - 4 * h + 1) * 128]
                        to_z(q).start()
            tile = acc[:, 0:128]
            for q in range(1, NZ):
                to_z(q).wait_recv()
                tile = tile + zbuf[q]
            if scalar:
                curve = acc[:, HALF:HALF + 128]
                for q in range(1, NZ):
                    scalar_z(q).wait_recv()
                    curve = curve + sbuf[q]
            else:
                curve = None
            tail(gap[...] * rows(d, m)[:, 0:128] + tile, curve)
            for q in range(1, NZ):
                to_z(q).wait_send()
            if scalar:
                for q in range(1, NZ):
                    scalar_z(q).wait_send()

        for h in (FAR, NEAR):
            for t in range(8):
                @pl.when(8 * c + t != m)
                def _():
                    to_chip(t, h).wait_send()
            pair(h).wait_send()

    def iterate(step, carry):
        def to_z(q):
            return remote(
                rows(img, m).at[:, 0:128], rows(img, m).at[:, q * 128:(q + 1) * 128],
                agz_s.at[q], agz_r.at[q], at_z(SHIFT[q]),
            )

        def tail(tile, curve):
            rows(img, m)[:, 0:128] = tile
            for q in range(NZ - 1, 0, -1):
                to_z(q).start()

        def ready(h):
            for q in range(4 * h, 4 * h + 4):
                if q > 0:
                    to_z(q).wait_recv()

        reduce(lambda: None, tail, False)
        spread(ready)

        @pl.when(owner)
        def _():
            for q in range(1, NZ):
                to_z(q).wait_send()

        image, trial = img[...], d[...]
        old = rr[0:1, 0:1]
        alpha = old / total(trial * image)
        x[...] = x[...] + alpha * rows(d, m)[:, 0:128]
        left = r[...] - alpha * image
        new = total(left * left)
        r[...] = left
        d[...] = left + (new / old) * trial
        rr[...] = jnp.broadcast_to(new, (8, 128))
        set_trial()
        lax.fori_loop(0, CHUNKS, inter, 0)
        return carry

    lax.fori_loop(0, ITERS - 1, iterate, 0)

    def add_curvature():
        own_d = rows(d, m)[:, 0:128]
        own_gap = total(gap[...] * own_d * own_d)
        curve = total(d[:, 0:HALF] * part[:, 0:HALF]) + total(d[:, HALF:V] * part[:, HALF + 128:W])
        curve = curve + jnp.where(owner, own_gap, jnp.zeros_like(own_gap))
        part[:, HALF:HALF + 128] = jnp.broadcast_to(curve, (128, 128))

    def hand(ref):
        return remote(ref, ref, fs.at[0], fs.at[1], partner)

    def last(tile, curve):
        fin[:, 0:128] = tile
        fin[:, 128:256] = curve
        hand(fin).start()
        hand(fin).wait_send()

    reduce(add_curvature, last, True)

    @pl.when(jnp.logical_not(owner))
    def _():
        hand(fin).wait_recv()

    alpha = rr[...] / fin[:, 128:256]
    answer = x[...] + alpha * rows(d, m)[:, 0:128]
    left = rows(r, m)[:, 0:128] - alpha * fin[:, 0:128]
    lower = c == 0
    out[0] = jnp.where(lower, answer[0:4], answer[4:8])
    out[1] = jnp.where(lower, left[0:4], left[4:8])

    for n in range(CHUNKS):
        for q in ISSUE:
            exchange(q, n).wait_send()


def on_device(integrals, occupied_energy, virtual_energy, right_side):
    dma = pltpu.SemaphoreType.DMA
    vmem = pl.BlockSpec(memory_space=pltpu.VMEM)
    result = pl.pallas_call(
        kernel,
        out_shape=jax.ShapeDtypeStruct((2, 4, 128), F32),
        in_specs=[pl.BlockSpec(memory_space=pl.ANY), pl.BlockSpec(memory_space=pltpu.SMEM), vmem, vmem],
        out_specs=vmem,
        scratch_shapes=[
            pltpu.VMEM((NZ, NP, 128, 128), F32),
            pltpu.VMEM((NP * O, V), BF16),
            pltpu.VMEM((NP * O, V), BF16),
            pltpu.VMEM((O, V), F32),
            pltpu.VMEM((O, V), F32),
            pltpu.VMEM((O, V), F32),
            pltpu.VMEM((O, W), F32),
            pltpu.VMEM((64, W), F32),
            pltpu.VMEM((NM, 8, W), F32),
            pltpu.VMEM((NZ, 8, 128), F32),
            pltpu.VMEM((NZ, 8, 128), F32),
            pltpu.VMEM((NZ, 8, 128), F32),
            pltpu.VMEM((8, W), F32),
            pltpu.VMEM((8, W), F32),
            pltpu.VMEM((8, 128), F32),
            pltpu.VMEM((8, 128), F32),
            pltpu.VMEM((256, V), BF16),
            pltpu.VMEM((256, NP * O), BF16),
            pltpu.VMEM((8, 128), F32),
            pltpu.VMEM((8, 256), F32),
            dma((NZ, CHUNKS)), dma((NZ, CHUNKS)), dma(()),
            dma((NZ,)), dma((NZ,)), dma((2,)),
            dma((NZ,)), dma((NZ,)), dma((2, NM)), dma((2, 8)), dma((2, 8)), dma((2, 8)),
            dma((2,)), dma((2,)), dma((2, 8)), dma((2, NM)), dma((NZ,)), dma((NZ,)), dma((NZ,)), dma((NZ,)), dma((2,)),
        ],
        compiler_params=pltpu.CompilerParams(
            collective_id=0, has_side_effects=True, vmem_limit_bytes=60 << 20
        ),
        name="solve",
    )(integrals, occupied_energy, virtual_energy.reshape(1, 128), right_side.T)
    return result[0].T, result[1].T


def solution(mesh):
    in_specs = (P("aux", None, "vir"), P("aux"), P("vir"), P("vir", "aux"))
    out_specs = (P("vir", "aux"), P("vir", "aux"))
    return jax.shard_map(
        on_device, mesh=mesh, in_specs=in_specs, out_specs=out_specs, check_vma=False
    )
```

time: 282 us -> 273 us (0.968)
  Pallas kernels: 278 us -> 271 us
    pallas_call x1, Pallas kernels: 278 us -> 271 us  [on_device(): pl.pallas_call(kernel, out_shape=jax.ShapeDtypeStruct((2, 4, 128), F32),...]
where the time goes in v2:
time: 273 us; the launch traced here: 272 us
  Pallas kernels  271 us (99%)
    pallas_call x1, Pallas kernels, on_device(): pl.pallas_call(kernel, out_shape=jax.ShapeDtypeStruct((2, 4, 128), F32),...  271 us

profile of v2, /device:TPU:1, one launch (start us, length us, event | category | flops | bytes accessed | tf_op | source)
XLA Modules:
  0.0 272.5 jit_solution(16907299738362014892)
XLA Ops:
  0.6 270.6 %solve.1 = f32[2,4,128]{2,1,0:T(4,128)} custom-call(f32[128,128,128]{2,1,0:T(8,128)} %ints.1, f32[4]{0:T(128)} %occ.1, f32[1,128]{1,0:T(1,128)} %bitcast.11, f32[4,128]{1,0:T(4,128)} %bitcast.10), custom_call_target="tpu_custom_call" | custom-call | tf_op jit(solution)/shard_map/solve/pallas_call | solution.py:380
  271.2 1.3 slice_bitcast_fusion

commit v3 on v2

v3 whole, which is shorter than its diff:
```python
import functools

import jax
import jax.numpy as jnp
from jax import lax
from jax.experimental import pallas as pl
from jax.experimental.pallas import tpu as pltpu
from jax.sharding import PartitionSpec as P

ITERS = 3
NZ = 8
NM = 16
NP = 16
O = 128
V = 1024
W = V + 128
MESH = pl.DeviceIdType.MESH
F32 = jnp.float32
BF16 = jnp.bfloat16
SHIFT = (0, 1, -1, 2, -2, 3, -3, 4)
ISSUE = (7, 5, 6, 3, 4, 1, 2)
HALF = 512
CHUNKS = 8
NC = NP // CHUNKS


def total(x):
    return jnp.sum(jnp.sum(x, axis=0, keepdims=True), axis=1, keepdims=True)


def split(x):
    high = x.astype(BF16)
    return high, (x - high.astype(F32)).astype(BF16)


def kernel(
    ints, occ_in, vir_in, rhs_in, out,
    occ, vir, rhs, recv, bhi, blo, d, r, img, part, cbuf, xbuf, zbuf, zsend, tbuf, sbuf, g, g2, gap, x, d2, zs, rr, fin,
    a2a_s, a2a_r, loc, iz_s, iz_r, ic, agx_s, agx_r, agc_s, agc_r,
    rsc_s, rsc_r, rsx_s, rsx_r, zz_s, zz_r, rsz_s, rsz_r, sc_s, sc_r, fs,
):
    a = lax.axis_index("aux")
    z = lax.axis_index("vir")
    c = lax.rem(a, 2)
    m = lax.div(a, 2)
    owner = lax.div(m, 8) == c
    partner = (2 * m + 1 - c, z)

    def at_z(k):
        return (a, lax.rem(z + k + NZ, NZ))

    def at_m(chip):
        return (2 * chip + c, z)

    def remote(src, dst, send, recv_sem, dev):
        return pltpu.make_async_remote_copy(
            src_ref=src, dst_ref=dst, send_sem=send, recv_sem=recv_sem, device_id=dev, device_id_type=MESH
        )

    def rows(ref, chip, count=8):
        return ref.at[pl.ds(pl.multiple_of(8 * chip, 8), count)]

    barrier = pltpu.get_barrier_semaphore()
    pl.semaphore_signal(barrier, inc=1, device_id=partner, device_id_type=MESH)
    for k in range(1, NZ):
        pl.semaphore_signal(barrier, inc=1, device_id=at_z(k), device_id_type=MESH)
    for j in range(1, NM):
        pl.semaphore_signal(barrier, inc=1, device_id=at_m(lax.rem(m + j, NM)), device_id_type=MESH)

    small = [
        pltpu.make_async_copy(source, target, loc.at[i])
        for i, (source, target) in enumerate(((occ_in, occ), (vir_in, vir), (rhs_in, rhs)), 1)
    ]
    for copy in small:
        copy.start()
    here = pl.ds(pl.multiple_of(z * 128, 128), 128)
    for copy in small:
        copy.wait()

    row = lax.broadcasted_iota(jnp.int32, (8, 128), 0)
    mine = lax.div(row, 4) == c
    occ_rows = jnp.zeros((8, 128), F32)
    for i in range(4):
        occ_rows = jnp.where(lax.rem(row, 4) == i, occ[i], occ_rows)
    own = rhs[...]
    g[0, :, here] = jnp.where(mine, jnp.concatenate([own, own], axis=0), 0.0)
    g[1, :, here] = jnp.where(mine, jnp.broadcast_to(vir[...], (8, 128)) - occ_rows, 0.0)

    pl.semaphore_wait(barrier, 1 + NZ - 1 + NM - 1)

    def init_z(q):
        tile = g.at[:, :, here]
        return remote(tile, tile, iz_s.at[q], iz_r.at[q], at_z(SHIFT[q]))

    def exchange(q, n):
        to = lax.rem(z + SHIFT[q] + NZ, NZ)
        return remote(
            ints.at[pl.ds(to * NP + n * NC, NC)], recv.at[z, pl.ds(n * NC, NC)], a2a_s.at[q, n], a2a_r.at[q, n], (a, to)
        )

    for q in range(1, NZ):
        init_z(q).start()
    for n in range(CHUNKS):
        for q in ISSUE:
            exchange(q, n).start()
    local = pltpu.make_async_copy(ints.at[pl.ds(z * NP, NP)], recv.at[z], loc.at[0])
    local.start()

    def spread(ready):
        def piece(chip, h):
            return rows(img, chip).at[:, h * HALF:(h + 1) * HALF]

        def to_chip(j, h):
            return remote(
                piece(m, h), piece(m, h), agx_s.at[h, j], agx_r.at[h, lax.rem(m, 8)], at_m(lax.rem(m + j, NM))
            )

        def to_partner(t, h):
            block = piece(8 * c + t, h)
            return remote(block, block, agc_s.at[h, t], agc_r.at[h, t], partner)

        def from_partner(t, h):
            block = piece(8 * (1 - c) + t, h)
            return remote(block, block, agc_s.at[h, t], agc_r.at[h, t], partner)

        @pl.when(owner)
        def _():
            for h in range(2):
                ready(h)
                for j in range(1, NM):
                    to_chip(j, h).start()
                to_partner(lax.rem(m, 8), h).start()

        for h in range(2):
            for t in range(8):
                @pl.when(8 * c + t != m)
                def _():
                    block = piece(8 * c + t, h)
                    remote(block, block, agx_s.at[0, 0], agx_r.at[h, t], partner).wait_recv()
                    to_partner(t, h).start()

        for h in range(2):
            for t in range(8):
                from_partner(t, h).wait_recv()
        for h in range(2):
            for t in range(8):
                to_partner(t, h).wait_send()

        @pl.when(owner)
        def _():
            for h in range(2):
                for j in range(1, NM):
                    to_chip(j, h).wait_send()

    for q in range(1, NZ):
        init_z(q).wait_recv()
    swap = remote(g, g2, ic.at[0], ic.at[1], partner)
    swap.start()
    swap.wait_recv()
    gap[...] = g[1] + g2[1]

    @pl.when(owner)
    def _():
        rows(img, m)[...] = g[0] + g2[0]

    spread(lambda h: None)
    swap.wait_send()
    for q in range(1, NZ):
        init_z(q).wait_send()

    first = img[...]
    d[...] = first
    r[...] = first
    rr[...] = jnp.broadcast_to(total(first * first), (8, 128))
    x[...] = jnp.zeros((8, 128), F32)

    def set_trial():
        high, low = split(d[...])
        d2[0:128, :] = high
        d2[128:256, :] = low

    def inter(n, count):
        eye = lax.broadcasted_iota(jnp.int32, (128, 128), 0) == lax.broadcasted_iota(jnp.int32, (128, 128), 1)
        contract = (((1,), (1,)), ((), ()))
        size = count * O
        at = pl.ds(pl.multiple_of(n * size, size), size)
        both = lax.dot_general(bhi[at, :], d2[...], contract, preferred_element_type=F32)
        rest = lax.dot_general(blo[at, :], d2[0:128, :], contract, preferred_element_type=F32)
        y = both[:, 0:128] + both[:, 128:256] + rest
        for i in range(count):
            block = y[i * 128:(i + 1) * 128, :]
            coulomb = total(jnp.where(eye, block, 0.0))
            zh, zl = split(jnp.where(eye, 4.0 * coulomb, 0.0) - block)
            cols = pl.ds(pl.multiple_of(n * size + i * 128, 128), 128)
            zs[0:128, cols] = zh
            zs[128:256, cols] = zl

    def outer(h):
        def body(n, carry):
            cols = pl.ds(pl.multiple_of(h * HALF + n * 256, 256), 256)
            to = pl.ds(pl.multiple_of(h * HALF + n * 256, 256), 256)
            both = jnp.dot(zs[...], bhi[:, cols], preferred_element_type=F32)
            rest = jnp.dot(zs[0:128, :], blo[:, cols], preferred_element_type=F32)
            part[:, to] = both[0:128] + both[128:256] + rest
            return carry

        lax.fori_loop(0, HALF // 256, body, 0)

    set_trial()
    local.wait()

    def arrive(n, carry):
        for q in ISSUE:
            exchange(q, n).wait_recv()

        def body(i, carry):
            p = n * NC + i
            at = pl.ds(pl.multiple_of(p * 128, 128), 128)
            for q in range(NZ):
                high, low = split(recv[q, p])
                bhi[at, q * 128:(q + 1) * 128] = high
                blo[at, q * 128:(q + 1) * 128] = low
            return carry

        lax.fori_loop(0, NC, body, 0)
        inter(n, NC)
        return carry

    lax.fori_loop(0, CHUNKS, arrive, 0)

    def span(h, scalar):
        return slice(h * HALF, W if h == 1 and scalar else (h + 1) * HALF)

    def reduce(before, collect, scalar):
        def pair(h):
            cols = span(h, scalar)
            theirs = rows(part, 8 * (1 - c), 64).at[:, cols]
            return remote(theirs, cbuf.at[:, cols], rsc_s.at[h], rsc_r.at[h], partner)

        def to_chip(t, h):
            chip = 8 * c + t
            j = lax.rem(chip - m + NM, NM)
            cols = span(h, scalar)
            return remote(
                rows(part, chip).at[:, cols], xbuf.at[j, :, cols], rsx_s.at[h, t], rsx_r.at[h, j], at_m(chip)
            )

        for h in range(2):
            outer(h)
            if h == 1:
                before()
            pair(h).start()
        for h in range(2):
            pair(h).wait_recv()
            cols = span(h, scalar)
            half = rows(part, 8 * c, 64)
            half[:, cols] = half[:, cols] + cbuf[:, cols]
            for t in range(8):
                @pl.when(8 * c + t != m)
                def _():
                    to_chip(t, h).start()

        @pl.when(owner)
        def _():
            for h in range(2):
                cols = span(h, scalar)
                acc = rows(part, m)[:, cols]
                for j in range(1, NM):
                    slot = xbuf.at[j, :, cols]
                    remote(slot, slot, rsx_s.at[0, 0], rsx_r.at[h, j], partner).wait_recv()
                    acc = acc + xbuf[j, :, cols]
                collect(h, acc)

        def finish():
            for h in range(2):
                for t in range(8):
                    @pl.when(8 * c + t != m)
                    def _():
                        to_chip(t, h).wait_send()
                pair(h).wait_send()

        return finish

    def iterate(step, carry):
        slot = lax.rem(step, 2)

        def to_z(q, h):
            block = zbuf.at[slot, z, :, h * HALF:(h + 1) * HALF]
            return remote(block, block, zz_s.at[slot, h, q], zz_r.at[slot, h, q], at_z(SHIFT[q]))

        def collect(h, acc):
            zbuf[slot, z, :, h * HALF:(h + 1) * HALF] = acc
            for q in ISSUE:
                to_z(q, h).start()

        def ready(h):
            cols = slice(h * HALF, (h + 1) * HALF)
            for q in range(1, NZ):
                to_z(q, h).wait_recv()
            acc = gap[:, cols] * rows(d, m)[:, cols]
            for s in range(NZ):
                acc = acc + zbuf[slot, s, :, cols]
            rows(img, m)[:, cols] = acc

        finish = reduce(lambda: None, collect, False)
        spread(ready)
        finish()

        @pl.when(owner)
        def _():
            for h in range(2):
                for q in range(1, NZ):
                    to_z(q, h).wait_send()

        image, trial = img[...], d[...]
        old = rr[0:1, 0:1]
        alpha = old / total(trial * image)
        x[...] = x[...] + alpha * rows(d, m)[:, here]
        left = r[...] - alpha * image
        new = total(left * left)
        r[...] = left
        d[...] = left + (new / old) * trial
        rr[...] = jnp.broadcast_to(new, (8, 128))
        set_trial()
        lax.fori_loop(0, NP // 4, lambda n, carry: inter(n, 4) or carry, 0)
        return carry

    lax.fori_loop(0, ITERS - 1, iterate, 0)

    own_d = rows(d, m)[:, here]

    def add_curvature():
        own_gap = total(gap[:, here] * own_d * own_d)
        curve = total(d[...] * part[:, 0:V]) + jnp.where(owner, own_gap, jnp.zeros_like(own_gap))
        part[:, V:W] = jnp.broadcast_to(curve, (128, 128))

    def tile_z(q):
        to = lax.rem(z + SHIFT[q] + NZ, NZ)
        return remote(zsend.at[to], tbuf.at[q], rsz_s.at[q], rsz_r.at[q], (a, to))

    def scalar_z(q):
        return remote(zsend.at[NZ], sbuf.at[q], sc_s.at[q], sc_r.at[q], at_z(SHIFT[q]))

    def hand(ref):
        return remote(ref, ref, fs.at[0], fs.at[1], partner)

    def last(h, acc):
        for s in range(4):
            zsend[4 * h + s] = acc[:, s * 128:(s + 1) * 128]
        if h == 0:
            return
        zsend[NZ] = acc[:, HALF:HALF + 128]
        for q in ISSUE:
            scalar_z(q).start()
            tile_z(q).start()
        tile = gap[:, here] * own_d + zsend[z]
        curve = zsend[NZ]
        for q in range(1, NZ):
            tile_z(q).wait_recv()
            scalar_z(q).wait_recv()
            tile = tile + tbuf[q]
            curve = curve + sbuf[q]
        fin[:, 0:128] = tile
        fin[:, 128:256] = curve
        hand(fin).start()
        for q in range(1, NZ):
            tile_z(q).wait_send()
            scalar_z(q).wait_send()
        hand(fin).wait_send()

    reduce(add_curvature, last, True)()

    @pl.when(jnp.logical_not(owner))
    def _():
        hand(fin).wait_recv()

    alpha = rr[...] / fin[:, 128:256]
    answer = x[...] + alpha * own_d
    left = rows(r, m)[:, here] - alpha * fin[:, 0:128]
    lower = c == 0
    out[0] = jnp.where(lower, answer[0:4], answer[4:8])
    out[1] = jnp.where(lower, left[0:4], left[4:8])

    for n in range(CHUNKS):
        for q in ISSUE:
            exchange(q, n).wait_send()


def on_device(integrals, occupied_energy, virtual_energy, right_side):
    dma = pltpu.SemaphoreType.DMA
    vmem = pl.BlockSpec(memory_space=pltpu.VMEM)
    result = pl.pallas_call(
        kernel,
        out_shape=jax.ShapeDtypeStruct((2, 4, 128), F32),
        in_specs=[pl.BlockSpec(memory_space=pl.ANY)] * 4,
        out_specs=vmem,
        scratch_shapes=[
            pltpu.SMEM((4,), F32),
            pltpu.VMEM((1, 128), F32),
            pltpu.VMEM((4, 128), F32),
            pltpu.VMEM((NZ, NP, 128, 128), F32),
            pltpu.VMEM((NP * O, V), BF16),
            pltpu.VMEM((NP * O, V), BF16),
            pltpu.VMEM((O, V), F32),
            pltpu.VMEM((O, V), F32),
            pltpu.VMEM((O, V), F32),
            pltpu.VMEM((O, W), F32),
            pltpu.VMEM((64, W), F32),
            pltpu.VMEM((NM, 8, W), F32),
            pltpu.VMEM((2, NZ, 8, V), F32),
            pltpu.VMEM((NZ + 1, 8, 128), F32),
            pltpu.VMEM((NZ, 8, 128), F32),
            pltpu.VMEM((NZ, 8, 128), F32),
            pltpu.VMEM((2, 8, V), F32),
            pltpu.VMEM((2, 8, V), F32),
            pltpu.VMEM((8, V), F32),
            pltpu.VMEM((8, 128), F32),
            pltpu.VMEM((256, V), BF16),
            pltpu.VMEM((256, NP * O), BF16),
            pltpu.VMEM((8, 128), F32),
            pltpu.VMEM((8, 256), F32),
            dma((NZ, CHUNKS)), dma((NZ, CHUNKS)), dma((4,)),
            dma((NZ,)), dma((NZ,)), dma((2,)), dma((2, NM)), dma((2, 8)), dma((2, 8)), dma((2, 8)),
            dma((2,)), dma((2,)), dma((2, 8)), dma((2, NM)), dma((2, 2, NZ)), dma((2, 2, NZ)),
            dma((NZ,)), dma((NZ,)), dma((NZ,)), dma((NZ,)), dma((2,)),
        ],
        compiler_params=pltpu.CompilerParams(
            collective_id=0, has_side_effects=True, vmem_limit_bytes=60 << 20
        ),
        name="solve",
    )(integrals, occupied_energy, virtual_energy.reshape(1, 128), right_side.T)
    return result[0].T, result[1].T


def solution(mesh):
    in_specs = (P("aux", None, "vir"), P("aux"), P("vir"), P("vir", "aux"))
    out_specs = (P("vir", "aux"), P("vir", "aux"))
    return jax.shard_map(
        on_device, mesh=mesh, in_specs=in_specs, out_specs=out_specs, check_vma=False
    )
```

time: 273 us -> 266 us (0.974)
  Pallas kernels: 271 us -> 264 us
    pallas_call x1, Pallas kernels: 271 us -> 264 us  [on_device(): pl.pallas_call(kernel, out_shape=jax.ShapeDtypeStruct((2, 4, 128), F32),...]
where the time goes in v3:
time: 266 us
  Pallas kernels  264 us (99%)
    pallas_call x1, Pallas kernels, on_device(): pl.pallas_call(kernel, out_shape=jax.ShapeDtypeStruct((2, 4, 128), F32),...  264 us

profile of v3, /device:TPU:1, one launch (start us, length us, event | category | flops | bytes accessed | tf_op | source)
XLA Modules:
  0.0 266.0 jit_solution(17055087913793969548)
XLA Ops:
  0.6 264.1 %solve.1 = f32[2,4,128]{2,1,0:T(4,128)} custom-call(f32[128,128,128]{2,1,0:T(8,128)} %ints.1, f32[4]{0:T(128)} %occ_in.1, f32[1,128]{1,0:T(1,128)} %bitcast.11, f32[4,128]{1,0:T(4,128)} %bitcast.10), custom_call_target="tpu_custom_call" | custom-call | tf_op jit(solution)/shard_map/solve/pallas_call | solution.py:392
  264.7 1.3 slice_bitcast_fusion

commit v4 on v3

--- a/solution.py
+++ b/solution.py
@@ -21,6 +21,7 @@
 ISSUE = (7, 5, 6, 3, 4, 1, 2)
 HALF = 512
 CHUNKS = 8
+AHEAD = 3
 NC = NP // CHUNKS
 
 
@@ -35,9 +36,9 @@
 
 def kernel(
     ints, occ_in, vir_in, rhs_in, out,
-    occ, vir, rhs, recv, bhi, blo, d, r, img, part, cbuf, xbuf, zbuf, zsend, tbuf, sbuf, g, g2, gap, x, d2, zs, rr, fin,
+    occ, vir, rhs, recv, bhi, blo, d, r, img, part, cbuf, xbuf, zbuf, zsend, tbuf, sbuf, g, g2, gap, x, d2, zs, rr,
     a2a_s, a2a_r, loc, iz_s, iz_r, ic, agx_s, agx_r, agc_s, agc_r,
-    rsc_s, rsc_r, rsx_s, rsx_r, zz_s, zz_r, rsz_s, rsz_r, sc_s, sc_r, fs,
+    rsc_s, rsc_r, rsx_s, rsx_r, zz_s, zz_r, rsz_s, rsz_r, sc_s, sc_r,
 ):
     a = lax.axis_index("aux")
     z = lax.axis_index("vir")
@@ -100,7 +101,7 @@
 
     for q in range(1, NZ):
         init_z(q).start()
-    for n in range(CHUNKS):
+    for n in range(AHEAD):
         for q in ISSUE:
             exchange(q, n).start()
     local = pltpu.make_async_copy(ints.at[pl.ds(z * NP, NP)], recv.at[z], loc.at[0])
@@ -211,6 +212,13 @@
 
     def arrive(n, carry):
         for q in ISSUE:
+            exchange(q, n).wait_send()
+
+            @pl.when(n + AHEAD < CHUNKS)
+            def _():
+                exchange(q, n + AHEAD).start()
+
+        for q in ISSUE:
             exchange(q, n).wait_recv()
 
         def body(i, carry):
@@ -322,7 +330,7 @@
         d[...] = left + (new / old) * trial
         rr[...] = jnp.broadcast_to(new, (8, 128))
         set_trial()
-        lax.fori_loop(0, NP // 4, lambda n, carry: inter(n, 4) or carry, 0)
+        lax.fori_loop(0, NP // 8, lambda n, carry: inter(n, 8) or carry, 0)
         return carry
 
     lax.fori_loop(0, ITERS - 1, iterate, 0)
@@ -334,15 +342,15 @@
         curve = total(d[...] * part[:, 0:V]) + jnp.where(owner, own_gap, jnp.zeros_like(own_gap))
         part[:, V:W] = jnp.broadcast_to(curve, (128, 128))
 
-    def tile_z(q):
+    def to_peers(q, core):
         to = lax.rem(z + SHIFT[q] + NZ, NZ)
-        return remote(zsend.at[to], tbuf.at[q], rsz_s.at[q], rsz_r.at[q], (a, to))
-
-    def scalar_z(q):
-        return remote(zsend.at[NZ], sbuf.at[q], sc_s.at[q], sc_r.at[q], at_z(SHIFT[q]))
-
-    def hand(ref):
-        return remote(ref, ref, fs.at[0], fs.at[1], partner)
+        dev = (2 * m + lax.rem(c + core, 2), to)
+        return (
+            remote(zsend.at[NZ], sbuf.at[q], sc_s.at[core, q], sc_r.at[q], dev),
+            remote(zsend.at[to], tbuf.at[q], rsz_s.at[core, q], rsz_r.at[q], dev),
+        )
+
+    sends = [(0, 1)] + [(q, core) for q in ISSUE for core in range(2)]
 
     def last(h, acc):
         for s in range(4):
@@ -350,40 +358,41 @@
         if h == 0:
             return
         zsend[NZ] = acc[:, HALF:HALF + 128]
-        for q in ISSUE:
-            scalar_z(q).start()
-            tile_z(q).start()
-        tile = gap[:, here] * own_d + zsend[z]
-        curve = zsend[NZ]
-        for q in range(1, NZ):
-            tile_z(q).wait_recv()
-            scalar_z(q).wait_recv()
-            tile = tile + tbuf[q]
-            curve = curve + sbuf[q]
-        fin[:, 0:128] = tile
-        fin[:, 128:256] = curve
-        hand(fin).start()
-        for q in range(1, NZ):
-            tile_z(q).wait_send()
-            scalar_z(q).wait_send()
-        hand(fin).wait_send()
-
-    reduce(add_curvature, last, True)()
+        for q, core in sends[1:] + sends[:1]:
+            for copy in to_peers(q, core):
+                copy.start()
+        tbuf[0] = zsend[z]
+        sbuf[0] = zsend[NZ]
+
+    finish = reduce(add_curvature, last, True)
 
     @pl.when(jnp.logical_not(owner))
     def _():
-        hand(fin).wait_recv()
-
-    alpha = rr[...] / fin[:, 128:256]
+        for copy in to_peers(0, 1):
+            copy.wait_recv()
+
+    tile = gap[:, here] * own_d + tbuf[0]
+    curve = sbuf[0]
+    for q in range(1, NZ):
+        for copy in to_peers(q, 0):
+            copy.wait_recv()
+        tile = tile + tbuf[q]
+        curve = curve + sbuf[q]
+
+    alpha = rr[...] / curve
     answer = x[...] + alpha * own_d
-    left = rows(r, m)[:, here] - alpha * fin[:, 0:128]
+    left = rows(r, m)[:, here] - alpha * tile
     lower = c == 0
     out[0] = jnp.where(lower, answer[0:4], answer[4:8])
     out[1] = jnp.where(lower, left[0:4], left[4:8])
 
-    for n in range(CHUNKS):
-        for q in ISSUE:
-            exchange(q, n).wait_send()
+    finish()
+
+    @pl.when(owner)
+    def _():
+        for q, core in sends:
+            for copy in to_peers(q, core):
+                copy.wait_send()
 
 
 def on_device(integrals, occupied_energy, virtual_energy, right_side):
@@ -418,11 +427,10 @@
             pltpu.VMEM((256, V), BF16),
             pltpu.VMEM((256, NP * O), BF16),
             pltpu.VMEM((8, 128), F32),
-            pltpu.VMEM((8, 256), F32),
             dma((NZ, CHUNKS)), dma((NZ, CHUNKS)), dma((4,)),
             dma((NZ,)), dma((NZ,)), dma((2,)), dma((2, NM)), dma((2, 8)), dma((2, 8)), dma((2, 8)),
             dma((2,)), dma((2,)), dma((2, 8)), dma((2, NM)), dma((2, 2, NZ)), dma((2, 2, NZ)),
-            dma((NZ,)), dma((NZ,)), dma((NZ,)), dma((NZ,)), dma((2,)),
+            dma((2, NZ)), dma((NZ,)), dma((2, NZ)), dma((NZ,)),
         ],
         compiler_params=pltpu.CompilerParams(
             collective_id=0, has_side_effects=True, vmem_limit_bytes=60 << 20

time: 266 us -> 264 us (level)
  no operation moved by 1% of the time
where the time goes in v4:
time: 264 us
  Pallas kernels  262 us (99%)
    pallas_call x1, Pallas kernels, on_device(): pl.pallas_call(kernel, out_shape=jax.ShapeDtypeStruct((2, 4, 128), F32),...  262 us

profile of v4, /device:TPU:1, one launch (start us, length us, event | category | flops | bytes accessed | tf_op | source)
XLA Modules:
  0.0 263.7 jit_solution(17780264517411963666)
XLA Ops:
  0.6 261.8 %solve.1 = f32[2,4,128]{2,1,0:T(4,128)} custom-call(f32[128,128,128]{2,1,0:T(8,128)} %ints.1, f32[4]{0:T(128)} %occ_in.1, f32[1,128]{1,0:T(1,128)} %bitcast.11, f32[4,128]{1,0:T(4,128)} %bitcast.10), custom_call_target="tpu_custom_call" | custom-call | tf_op jit(solution)/shard_map/solve/pallas_call | solution.py:401
  262.5 1.3 slice_bitcast_fusion

commit v5 on v4

--- a/solution.py
+++ b/solution.py
@@ -198,14 +198,14 @@
 
     def outer(h):
         def body(n, carry):
-            cols = pl.ds(pl.multiple_of(h * HALF + n * 256, 256), 256)
-            to = pl.ds(pl.multiple_of(h * HALF + n * 256, 256), 256)
+            cols = pl.ds(pl.multiple_of(h * HALF + n * HALF, 256), HALF)
+            to = pl.ds(pl.multiple_of(h * HALF + n * HALF, 256), HALF)
             both = jnp.dot(zs[...], bhi[:, cols], preferred_element_type=F32)
             rest = jnp.dot(zs[0:128, :], blo[:, cols], preferred_element_type=F32)
             part[:, to] = both[0:128] + both[128:256] + rest
             return carry
 
-        lax.fori_loop(0, HALF // 256, body, 0)
+        body(0, 0)
 
     set_trial()
     local.wait()
@@ -330,7 +330,7 @@
         d[...] = left + (new / old) * trial
         rr[...] = jnp.broadcast_to(new, (8, 128))
         set_trial()
-        lax.fori_loop(0, NP // 8, lambda n, carry: inter(n, 8) or carry, 0)
+        inter(0, NP)
         return carry
 
     lax.fori_loop(0, ITERS - 1, iterate, 0)

time: 264 us -> 263 us (level)
  no operation moved by 1% of the time
where the time goes in v5:
time: 263 us
  Pallas kernels  261 us (99%)
    pallas_call x1, Pallas kernels, on_device(): pl.pallas_call(kernel, out_shape=jax.ShapeDtypeStruct((2, 4, 128), F32),...  261 us

profile of v5, /device:TPU:1, one launch (start us, length us, event | category | flops | bytes accessed | tf_op | source)
XLA Modules:
  0.0 262.7 jit_solution(16078739119459337500)
XLA Ops:
  0.6 260.8 %solve.1 = f32[2,4,128]{2,1,0:T(4,128)} custom-call(f32[128,128,128]{2,1,0:T(8,128)} %ints.1, f32[4]{0:T(128)} %occ_in.1, f32[1,128]{1,0:T(1,128)} %bitcast.11, f32[4,128]{1,0:T(4,128)} %bitcast.10), custom_call_target="tpu_custom_call" | custom-call | tf_op jit(solution)/shard_map/solve/pallas_call | solution.py:401
  261.4 1.3 slice_bitcast_fusion
